TPU v7x, 32 devices: a whole 2x2x4 slice. The times are simulated.
32 devices in a mesh: seq: 8 (over y, x, core), tp: 4 (over z).
Axes of the slice: x: 2, y: 2, z: 4, core: 2. Of those that a mesh axis runs over, the one named last changes fastest.
Arguments:
- tokens: bfloat16 [128, 17, 1152], P('seq'), may hold values from -6 to 6
- cotangent: bfloat16 [128, 17, 1152], P('seq'), may hold values from -6 to 6
- caption: bfloat16 [4, 300, 1152], replicated, may hold values from -6 to 6
- condition: float32 [4, 1152], replicated, may hold values from -6 to 6
- frames: int32 [4], replicated, may hold values from 1 to 17, 44 in all
- cap_len: int32 [4], replicated, may hold values from 1 to 300, 600 in all
- clip_of: int32 [128], P('seq'), may hold values from 0 to 3
- w_qkv: bfloat16 [1152, 3, 1152], P('seq', None, 'tp'), may hold values from -0.1875 to 0.1875
- w_out: bfloat16 [1152, 1152], P('tp', 'seq'), may hold values from -0.375 to 0.375
- w_query2: bfloat16 [1152, 1152], P('seq', 'tp'), may hold values from -0.1875 to 0.1875
- w_kv2: bfloat16 [1152, 2, 1152], P('seq', None, 'tp'), may hold values from -0.1875 to 0.1875
- w_out2: bfloat16 [1152, 1152], P('tp', 'seq'), may hold values from -0.75 to 0.75
- w_up: bfloat16 [1152, 4608], P('seq', 'tp'), may hold values from -0.1875 to 0.1875
- w_down: bfloat16 [4608, 1152], P('tp', 'seq'), may hold values from -0.09375 to 0.09375
- w_ada: bfloat16 [1152, 6912], P('seq', 'tp'), may hold values from -0.1875 to 0.1875
Outputs:
- output: bfloat16 [128, 17, 1152], P('seq')
- d_tokens: bfloat16 [128, 17, 1152], P('seq')
- d_caption: float32 [4, 300, 1152], P(None, None, 'tp')
- d_condition: float32 [4, 1152], replicated
- d_w_qkv: float32 [1152, 3, 1152], P('seq', None, 'tp')
- d_w_out: float32 [1152, 1152], P('tp', 'seq')
- d_w_query2: float32 [1152, 1152], P('seq', 'tp')
- d_w_kv2: float32 [1152, 2, 1152], P('seq', None, 'tp')
- d_w_out2: float32 [1152, 1152], P('tp', 'seq')
- d_w_up: float32 [1152, 4608], P('seq', 'tp')
- d_w_down: float32 [4608, 1152], P('tp', 'seq')
- d_w_ada: float32 [1152, 6912], P('seq', 'tp')
Inputs may be any that keep to these rules, and one draw needn't show every extreme that they name: frames of each clip; they add up to 44 and one clip has 17. `cap_len`: live caption tokens of each clip, the first ones of its slots; they add up to 600 and one clip has 300.
All inputs are finite; a program needn't handle non-finite values.
Results may differ from a plain program's by a relative error of at most 0.024.
Values may be sent and summed in bfloat16 or wider, within the bound.
No kernel may reach another device: no remote copies, remote signals or barrier semaphores. Data moves between devices by JAX's collectives and lax.ppermute only.
A program may use at most 128 MiB of HBM per device.

v0:
```python
import jax
import jax.numpy as jnp
from jax import lax
from jax.sharding import PartitionSpec as P

HDIM = 72
CLIPS = 4
EPSILON = 1e-06
NEG_FILL = -1e30
HIGHEST = lax.Precision.HIGHEST


def normalize(rows):
    center = rows - jnp.mean(rows, -1, keepdims=True)
    return center * lax.rsqrt(jnp.mean(center * center, -1, keepdims=True) + EPSILON)


def modulate(rows, shift, scale):
    return normalize(rows) * (1.0 + scale[:, None, :]) + shift[:, None, :]


def total_rows(partial_value):
    return lax.psum(partial_value, "tp")


def frame_attention(triple, live, head_scale):
    raw = (
        jnp.einsum(
            "lfhe,lghe->lhfg", triple[:, :, 0], triple[:, :, 1], preferred_element_type=jnp.float32
        )
        * head_scale
    )
    probs = jax.nn.softmax(jnp.where(live[:, None, None, :], raw, NEG_FILL), axis=-1)
    result = jnp.einsum(
        "lhfg,lghe->lfhe",
        probs.astype(jnp.bfloat16),
        triple[:, :, 2],
        preferred_element_type=jnp.float32,
    )
    return (probs, result.astype(jnp.bfloat16))


def cross_scores(query, keys, clips, key_clip, key_live, head_scale):
    raw = jnp.einsum("rhe,khe->hrk", query, keys, preferred_element_type=jnp.float32) * head_scale
    allowed = (clips[:, None] == key_clip[None, :]) & key_live[None, :]
    return jnp.where(allowed[None], raw, NEG_FILL)


def shards(
    tokens,
    cotangent,
    caption,
    condition,
    frames,
    cap_len,
    clip_of,
    w_qkv,
    w_out,
    w_query2,
    w_kv2,
    w_out2,
    w_up,
    w_down,
    w_ada,
):
    seqs, fmax, width = tokens.shape
    row_count = seqs * fmax
    inner = w_qkv.shape[2]
    local_heads = inner // HDIM
    head_scale = HDIM ** (-0.5)
    full_qkv, full_out, full_query2, full_kv2, full_out2, full_up, full_down, full_ada = (
        lax.all_gather(w_qkv, "seq", axis=0, tiled=True),
        lax.all_gather(w_out, "seq", axis=1, tiled=True),
        lax.all_gather(w_query2, "seq", axis=0, tiled=True),
        lax.all_gather(w_kv2, "seq", axis=0, tiled=True),
        lax.all_gather(w_out2, "seq", axis=1, tiled=True),
        lax.all_gather(w_up, "seq", axis=0, tiled=True),
        lax.all_gather(w_down, "seq", axis=1, tiled=True),
        lax.all_gather(w_ada, "seq", axis=0, tiled=True),
    )
    qkv_matrix = full_qkv.reshape(width, 3 * inner)
    kv_matrix = full_kv2.reshape(width, 2 * inner)
    scaled = jax.nn.silu(condition).astype(jnp.bfloat16)
    mod_part = jnp.dot(scaled, full_ada, preferred_element_type=jnp.float32)
    mods = lax.all_gather(mod_part, "tp", axis=1, tiled=True).reshape(CLIPS, 6, width)
    clip_ids = jnp.arange(CLIPS)
    clip_hot = clip_of[:, None] == clip_ids[None, :]
    seq_mods = jnp.sum(jnp.where(clip_hot[:, :, None, None], mods[None], 0.0), 1)
    seq_frames = jnp.sum(jnp.where(clip_hot, frames[None, :], 0), 1)
    live = jnp.arange(fmax)[None, :] < seq_frames[:, None]
    own_live = live.astype(jnp.float32)[:, :, None]
    own_hot = clip_hot.astype(jnp.float32)
    key_count = caption.shape[0] * caption.shape[1]
    key_clip = jnp.arange(key_count) // caption.shape[1]
    key_len = jnp.sum(jnp.where(key_clip[:, None] == clip_ids[None, :], cap_len[None, :], 0), 1)
    key_live = jnp.arange(key_count) % caption.shape[1] < key_len
    row_clip = jnp.repeat(clip_of, fmax)
    block_seqs = min(32, seqs)
    blocks = seqs // block_seqs
    block_rows = block_seqs * fmax
    block_clip = row_clip.reshape(blocks, block_rows)
    own_input = tokens.astype(jnp.float32)
    attn_in = (
        modulate(own_input, seq_mods[:, 0], seq_mods[:, 1])
        .astype(jnp.bfloat16)
        .reshape(row_count, width)
    )
    triple = (
        jnp.dot(attn_in, qkv_matrix, preferred_element_type=jnp.float32)
        .astype(jnp.bfloat16)
        .reshape(seqs, fmax, 3, local_heads, HDIM)
    )
    probs, frame_out = frame_attention(triple, live, head_scale)
    frame_out = frame_out.reshape(row_count, inner)
    branch_one = total_rows(
        jnp.dot(frame_out, full_out, preferred_element_type=jnp.float32).reshape(seqs, fmax, width)
    )
    first = own_input + seq_mods[:, 2][:, None, :] * branch_one
    first_low = first.astype(jnp.bfloat16).reshape(row_count, width)
    cross_query = (
        jnp.dot(first_low, full_query2, preferred_element_type=jnp.float32)
        .astype(jnp.bfloat16)
        .reshape(blocks, block_rows, local_heads, HDIM)
    )
    cross_kv = (
        jnp.dot(caption.reshape(key_count, width), kv_matrix, preferred_element_type=jnp.float32)
        .astype(jnp.bfloat16)
        .reshape(key_count, 2, local_heads, HDIM)
    )
    cross_key = cross_kv[:, 0]
    cross_value = cross_kv[:, 1]

    def cross_block(pair):
        query, clips = pair
        scores = cross_scores(query, cross_key, clips, key_clip, key_live, head_scale)
        top = jnp.max(scores, -1, keepdims=True)
        weights = jnp.exp(scores - top)
        denom = jnp.sum(weights, -1, keepdims=True)
        block_out = jnp.einsum(
            "hrk,khe->rhe",
            (weights / denom).astype(jnp.bfloat16),
            cross_value,
            preferred_element_type=jnp.float32,
        )
        return (block_out.astype(jnp.bfloat16), (top + jnp.log(denom))[..., 0])

    cross_out, cross_lse = lax.map(cross_block, (cross_query, block_clip))
    cross_out = cross_out.reshape(row_count, inner)
    second = first + total_rows(
        jnp.dot(cross_out, full_out2, preferred_element_type=jnp.float32).reshape(seqs, fmax, width)
    )
    mlp_in = (
        modulate(second, seq_mods[:, 3], seq_mods[:, 4])
        .astype(jnp.bfloat16)
        .reshape(row_count, width)
    )
    hidden_pre = jnp.dot(mlp_in, full_up, preferred_element_type=jnp.float32)
    hidden = jax.nn.gelu(hidden_pre, approximate=True).astype(jnp.bfloat16)
    branch_three = total_rows(
        jnp.dot(hidden, full_down, preferred_element_type=jnp.float32).reshape(seqs, fmax, width)
    )
    third = second + seq_mods[:, 5][:, None, :] * branch_three
    output = (third * own_live).astype(jnp.bfloat16)
    grad_three = cotangent.astype(jnp.float32) * own_live
    d_branch3 = (
        (seq_mods[:, 5][:, None, :] * grad_three).astype(jnp.bfloat16).reshape(row_count, width)
    )
    grad_down = jnp.einsum("rk,rd->kd", hidden, d_branch3, preferred_element_type=jnp.float32)
    d_hidden = jnp.einsum("rd,kd->rk", d_branch3, full_down, preferred_element_type=jnp.float32)
    gelu_pull = jax.vjp(lambda value: jax.nn.gelu(value, approximate=True), hidden_pre)[1]
    d_pre = gelu_pull(d_hidden)[0].astype(jnp.bfloat16)
    grad_up = jnp.einsum("rd,rk->dk", mlp_in, d_pre, preferred_element_type=jnp.float32)
    d_mlp = total_rows(
        jnp.einsum("rk,dk->rd", d_pre, full_up, preferred_element_type=jnp.float32).reshape(
            seqs, fmax, width
        )
    )
    second_pull = jax.vjp(modulate, second, seq_mods[:, 3], seq_mods[:, 4])[1]
    norm_two, d_shift2, d_scale2 = second_pull(d_mlp)
    grad_two = grad_three + norm_two
    d_branch2 = grad_two.astype(jnp.bfloat16).reshape(row_count, width)
    grad_out2 = jnp.einsum("rc,rd->cd", cross_out, d_branch2, preferred_element_type=jnp.float32)
    d_cross = (
        jnp.einsum("rd,cd->rc", d_branch2, full_out2, preferred_element_type=jnp.float32)
        .astype(jnp.bfloat16)
        .reshape(blocks, block_rows, local_heads, HDIM)
    )

    def cross_back(carry, item):
        key_sum, value_sum = carry
        query, clips, block_lse, grad_block = item
        scores = cross_scores(query, cross_key, clips, key_clip, key_live, head_scale)
        weights = jnp.exp(scores - block_lse[..., None])
        value_sum = value_sum + jnp.einsum(
            "hrk,rhe->khe",
            weights.astype(jnp.bfloat16),
            grad_block,
            preferred_element_type=jnp.float32,
        )
        grad_weights = jnp.einsum(
            "rhe,khe->hrk", grad_block, cross_value, preferred_element_type=jnp.float32
        )
        grad_scores = (
            weights * (grad_weights - jnp.sum(weights * grad_weights, -1, keepdims=True))
        ).astype(jnp.bfloat16)
        grad_query = (
            jnp.einsum("hrk,khe->rhe", grad_scores, cross_key, preferred_element_type=jnp.float32)
            * head_scale
        ).astype(jnp.bfloat16)
        key_sum = (
            key_sum
            + jnp.einsum("hrk,rhe->khe", grad_scores, query, preferred_element_type=jnp.float32)
            * head_scale
        )
        return ((key_sum, value_sum), grad_query)

    zero_keys = jnp.zeros((key_count, local_heads, HDIM), jnp.float32)
    (key_grad, value_grad), d_query = lax.scan(
        cross_back, (zero_keys, zero_keys), (cross_query, block_clip, cross_lse, d_cross)
    )
    d_query = d_query.reshape(row_count, inner)
    grad_query2 = jnp.einsum("rd,rc->dc", first_low, d_query, preferred_element_type=jnp.float32)
    grad_one = grad_two + total_rows(
        jnp.einsum("rc,dc->rd", d_query, full_query2, preferred_element_type=jnp.float32).reshape(
            seqs, fmax, width
        )
    )
    d_branch1 = (
        (seq_mods[:, 2][:, None, :] * grad_one).astype(jnp.bfloat16).reshape(row_count, width)
    )
    grad_out = jnp.einsum("rc,rd->cd", frame_out, d_branch1, preferred_element_type=jnp.float32)
    d_frame = (
        jnp.einsum("rd,cd->rc", d_branch1, full_out, preferred_element_type=jnp.float32)
        .astype(jnp.bfloat16)
        .reshape(seqs, fmax, local_heads, HDIM)
    )
    d_value = jnp.einsum(
        "lhfg,lfhe->lghe", probs.astype(jnp.bfloat16), d_frame, preferred_element_type=jnp.float32
    )
    d_probs = jnp.einsum(
        "lfhe,lghe->lhfg", d_frame, triple[:, :, 2], preferred_element_type=jnp.float32
    )
    d_scores = (probs * (d_probs - jnp.sum(probs * d_probs, -1, keepdims=True))).astype(
        jnp.bfloat16
    )
    d_queries = (
        jnp.einsum("lhfg,lghe->lfhe", d_scores, triple[:, :, 1], preferred_element_type=jnp.float32)
        * head_scale
    )
    d_keys = (
        jnp.einsum("lhfg,lfhe->lghe", d_scores, triple[:, :, 0], preferred_element_type=jnp.float32)
        * head_scale
    )
    d_triple = (
        jnp.stack([d_queries, d_keys, d_value], 2)
        .astype(jnp.bfloat16)
        .reshape(row_count, 3 * inner)
    )
    grad_qkv = jnp.einsum(
        "rd,rc->dc", attn_in, d_triple, preferred_element_type=jnp.float32
    ).reshape(width, 3, inner)
    d_attn = total_rows(
        jnp.einsum("rc,dc->rd", d_triple, qkv_matrix, preferred_element_type=jnp.float32).reshape(
            seqs, fmax, width
        )
    )
    first_pull = jax.vjp(modulate, own_input, seq_mods[:, 0], seq_mods[:, 1])[1]
    norm_one, d_shift1, d_scale1 = first_pull(d_attn)
    d_tokens = (grad_one + norm_one).astype(jnp.bfloat16)
    d_gate1 = jnp.sum(grad_one * branch_one, 1)
    d_gate2 = jnp.sum(grad_three * branch_three, 1)
    seq_terms = jnp.stack([d_shift1, d_scale1, d_gate1, d_shift2, d_scale2, d_gate2], 1)
    d_mods = jnp.einsum("lc,ljd->cjd", own_hot, seq_terms, precision=HIGHEST).reshape(
        CLIPS, 6 * width
    )
    kv_grad = jnp.stack([key_grad, value_grad], 1)
    kv_total, mods_total = (
        lax.psum(kv_grad.astype(jnp.bfloat16), "seq").astype(jnp.float32),
        lax.psum(d_mods.astype(jnp.bfloat16), "seq").astype(jnp.float32),
    )
    col_count = mods_total.shape[1] // lax.axis_size("tp")
    mod_cols = lax.dynamic_slice_in_dim(mods_total, lax.axis_index("tp") * col_count, col_count, 1)
    seq_rows = w_ada.shape[0]
    seq_start = lax.axis_index("seq") * seq_rows
    scaled_rows = lax.dynamic_slice_in_dim(scaled, seq_start, seq_rows, 1).astype(jnp.float32)
    grad_ada = jnp.einsum("cd,ck->dk", scaled_rows, mod_cols, precision=HIGHEST)
    silu_pull = jax.vjp(jax.nn.silu, condition)[1]
    cond_part = silu_pull(
        jnp.einsum("ck,dk->cd", mod_cols, full_ada.astype(jnp.float32), precision=HIGHEST)
    )[0]
    d_condition = lax.psum(cond_part, "tp")
    kv_low = kv_total.astype(jnp.bfloat16).reshape(key_count, 2 * inner)
    caption_rows = lax.dynamic_slice_in_dim(
        caption.reshape(key_count, width), seq_start, seq_rows, 1
    )
    grad_kv2 = jnp.einsum(
        "kd,kc->dc", caption_rows, kv_low, preferred_element_type=jnp.float32
    ).reshape(seq_rows, 2, inner)
    caption_part = jnp.einsum(
        "kc,dc->kd", kv_low, kv_matrix, preferred_element_type=jnp.float32
    ).reshape(caption.shape)
    d_caption = lax.psum_scatter(
        caption_part.astype(jnp.bfloat16), "tp", scatter_dimension=2, tiled=True
    ).astype(jnp.float32)
    summed = (
        lax.psum_scatter(
            grad_qkv.astype(jnp.bfloat16), "seq", scatter_dimension=0, tiled=True
        ).astype(jnp.float32),
        lax.psum_scatter(
            grad_out.astype(jnp.bfloat16), "seq", scatter_dimension=1, tiled=True
        ).astype(jnp.float32),
        lax.psum_scatter(
            grad_query2.astype(jnp.bfloat16), "seq", scatter_dimension=0, tiled=True
        ).astype(jnp.float32),
        lax.psum_scatter(
            grad_out2.astype(jnp.bfloat16), "seq", scatter_dimension=1, tiled=True
        ).astype(jnp.float32),
        lax.psum_scatter(
            grad_up.astype(jnp.bfloat16), "seq", scatter_dimension=0, tiled=True
        ).astype(jnp.float32),
        lax.psum_scatter(
            grad_down.astype(jnp.bfloat16), "seq", scatter_dimension=1, tiled=True
        ).astype(jnp.float32),
    )
    return (
        output,
        d_tokens,
        d_caption,
        d_condition,
        summed[0],
        summed[1],
        summed[2],
        grad_kv2,
        summed[3],
        summed[4],
        summed[5],
        grad_ada,
    )


def solution(mesh):
    return jax.shard_map(
        shards,
        mesh=mesh,
        in_specs=(
            P("seq", None, None),
            P("seq", None, None),
            P(),
            P(),
            P(),
            P(),
            P("seq"),
            P("seq", None, "tp"),
            P("tp", "seq"),
            P("seq", "tp"),
            P("seq", None, "tp"),
            P("tp", "seq"),
            P("seq", "tp"),
            P("tp", "seq"),
            P("seq", "tp"),
        ),
        out_specs=(
            P("seq", None, None),
            P("seq", None, None),
            P(None, None, "tp"),
            P(),
            P("seq", None, "tp"),
            P("tp", "seq"),
            P("seq", "tp"),
            P("seq", None, "tp"),
            P("tp", "seq"),
            P("seq", "tp"),
            P("tp", "seq"),
            P("seq", "tp"),
        ),
        check_vma=False,
    )
```

profile of v0, /device:TPU:0, one launch (start us, length us, event | category | flops | bytes accessed | tf_op | source)
XLA Modules:
  0.0 1068.3 jit_solution(13612882484881826433)
XLA Ops:
  14.8 15.0 %all_gather.30 = bf16[288,1152]{0,1:T(8,128)(2,1)S(1)} all-gather(bf16[288,144]{0,1:T(8,128)(2,1)S(1)} %copy-done.45), channel_id=1, replica_groups=mesh['seq'=8,'tp'=4] {'seq'}, dimensions={1}, use_global_device_ids=true | all-gather | bytes 746496 | tf_op jit(solution)/shard_map/all_gather | solution.py:73
  29.7 13.7 %all_gather.32 = bf16[1152,288]{1,0:T(8,128)(2,1)S(1)} all-gather(bf16[144,288]{1,0:T(8,128)(2,1)S(1)} %copy-done.46), channel_id=1, replica_groups=mesh['seq'=8,'tp'=4] {'seq'}, dimensions={0}, use_global_device_ids=true | all-gather | bytes 746496 | tf_op jit(solution)/shard_map/all_gather | solution.py:74
  43.4 11.3 %all_gather.33 = bf16[288,1152]{0,1:T(8,128)(2,1)} all-gather(bf16[288,144]{0,1:T(8,128)(2,1)S(1)} %copy-done.47), channel_id=1, replica_groups=mesh['seq'=8,'tp'=4] {'seq'}, dimensions={1}, use_global_device_ids=true | all-gather | bytes 746496 | tf_op jit(solution)/shard_map/all_gather | solution.py:76
  64.2 21.8 %all-gather.7.cloned.1.call-done = bf16[1152,1728]{1,0:T(8,128)(2,1)} async-done(((bf16[144,1728]{1,0:T(8,128)(2,1)}), bf16[1152,1728]{1,0:T(8,128)(2,1)}) %all-gather.7.cloned.1.call-update) | async-done | bytes 3981328 | tf_op jit(solution)/shard_map/all_gather | solution.py:79
  88.8 13.4 %all-gather = f32[4,1728,4]{1,2,0:T(4,128)S(1)} all-gather(f32[1,1728,4]{1,2,0:T(4,128)S(1)} %convolution_bitcast_fusion), channel_id=1, replica_groups=mesh['seq'=8,'tp'=4] {'tp'}, dimensions={0}, use_global_device_ids=true | all-gather | bytes 138240 | tf_op jit(solution)/shard_map/all_gather | solution.py:85
  123.3 5.6 copy.152
  128.9 5.6 convolution_convert_fusion.4
  134.5 63.4 %all-reduce.8.cloned.1.call-done = f32[16,17,1152]{2,1,0:T(8,128)} async-done(((f32[16,17,1152]{2,1,0:T(8,128)}), f32[16,17,1152]{2,1,0:T(8,128)}) %all-reduce.8.cloned.1.call-update) | async-done | bytes 1253392 | tf_op jit(solution)/shard_map/psum | solution.py:23
  212.2 73.3 %all-reduce.10.cloned.1.call-done = f32[16,17,1152]{2,1,0:T(8,128)} async-done(((f32[16,17,1152]{2,1,0:T(8,128)}), f32[16,17,1152]{2,1,0:T(8,128)}) %all-reduce.10.cloned.1.call-update) | async-done | bytes 1253392 | tf_op jit(solution)/shard_map/psum | solution.py:23
  295.4 21.2 %all-gather.15.cloned.1.call-done = bf16[1152,1152]{0,1:T(8,128)(2,1)} async-done(((bf16[1152,144]{0,1:T(8,128)(2,1)}), bf16[1152,1152]{0,1:T(8,128)(2,1)}) %all-gather.15.cloned.1.call-update) | async-done | bytes 2654224 | tf_op jit(solution)/shard_map/all_gather | solution.py:78
  320.7 28.1 %all-gather.13.cloned.1.call-done = bf16[1152,1152]{1,0:T(8,128)(2,1)} async-done(((bf16[144,1152]{1,0:T(8,128)(2,1)}), bf16[1152,1152]{1,0:T(8,128)(2,1)}) %all-gather.13.cloned.1.call-update) | async-done | bytes 2654224 | tf_op jit(solution)/shard_map/all_gather | solution.py:77
  348.8 5.0 fusion.36
  359.8 75.4 %all-reduce.12.cloned.1.call-done = f32[16,17,1152]{2,1,0:T(8,128)} async-done(((f32[16,17,1152]{2,1,0:T(8,128)}), f32[16,17,1152]{2,1,0:T(8,128)}) %all-reduce.12.cloned.1.call-update) | async-done | bytes 1253392 | tf_op jit(solution)/shard_map/psum | solution.py:23
  476.0 59.8 %all-reduce.14.cloned.1.call-done = f32[16,17,1152]{2,1,0:T(8,128)} async-done(((f32[16,17,1152]{2,1,0:T(8,128)}), f32[16,17,1152]{2,1,0:T(8,128)}) %all-reduce.14.cloned.1.call-update) | async-done | bytes 1253392 | tf_op jit(solution)/shard_map/psum | solution.py:23
  604.5 6.6 convolution_convert_fusion.2
  611.1 23.5 %reduce-scatter.16.cloned.1.call-done = bf16[288,144]{0,1:T(8,128)(2,1)} async-done(((bf16[288,1152]{0,1:T(8,128)(2,1)}), bf16[288,144]{0,1:T(8,128)(2,1)}) %reduce-scatter.16.cloned.1.call-update) | async-done | bytes 82960 | tf_op jit(solution)/shard_map/reduce_scatter | solution.py:315
  636.2 36.7 %reduce-scatter.14.cloned.1.call-done = bf16[144,288]{1,0:T(8,128)(2,1)} async-done(((bf16[1152,288]{1,0:T(8,128)(2,1)}), bf16[144,288]{1,0:T(8,128)(2,1)}) %reduce-scatter.14.cloned.1.call-update) | async-done | bytes 82960 | tf_op jit(solution)/shard_map/reduce_scatter | solution.py:312
  674.4 37.7 %reduce-scatter.12.cloned.1.call-done = bf16[288,144]{0,1:T(8,128)(2,1)} async-done(((bf16[288,1152]{0,1:T(8,128)(2,1)}), bf16[288,144]{0,1:T(8,128)(2,1)}) %reduce-scatter.12.cloned.1.call-update) | async-done | bytes 82960 | tf_op jit(solution)/shard_map/reduce_scatter | solution.py:309
  713.7 45.6 %reduce-scatter.18.cloned.1.call-done = bf16[144,1152]{1,0:T(8,128)(2,1)} async-done(((bf16[1152,1152]{1,0:T(8,128)(2,1)}), bf16[144,1152]{1,0:T(8,128)(2,1)}) %reduce-scatter.18.cloned.1.call-update) | async-done | bytes 331792 | tf_op jit(solution)/shard_map/reduce_scatter | solution.py:318
  761.2 45.7 %reduce-scatter.20.cloned.1.call-done = bf16[1152,144]{0,1:T(8,128)(2,1)} async-done(((bf16[1152,1152]{0,1:T(8,128)(2,1)}), bf16[1152,144]{0,1:T(8,128)(2,1)}) %reduce-scatter.20.cloned.1.call-update) | async-done | bytes 331792 | tf_op jit(solution)/shard_map/reduce_scatter | solution.py:321
  808.7 135.2 %all-reduce.18.cloned.1.call-done = (f32[16,17,1152]{2,1,0:T(8,128)}, f32[16,17,1152]{2,1,0:T(8,128)}) async-done(((f32[16,17,1152]{2,1,0:T(8,128)}, f32[16,17,1152]{2,1,0:T(8,128)}), (f32[16,17,1152]{2,1,0:T(8,128)}, f32[16,17,1152]{2,1,0:T(8,128)})) %all-reduce.18.cloned.1.call-update) | async-done | bytes 2506768 | tf_op jit(solution)/shard_map/psum | solution.py:23
  951.2 24.9 %psum.70 = bf16[4,6912]{1,0:T(4,128)(2,1)S(1)} all-reduce(bf16[4,6912]{1,0:T(4,128)(2,1)S(1)} %bitcast.198), channel_id=1, replica_groups=mesh['seq'=8,'tp'=4] {'seq'}, use_global_device_ids=true, to_apply=%region_31.32 | all-reduce | flops 27648 | bytes 110592 | tf_op jit(solution)/shard_map/psum | solution.py:279
  979.5 17.6 %psum.71 = f32[4,1152]{1,0:T(4,128)} all-reduce(f32[4,1152]{1,0:T(4,128)S(1)} %fusion.68), channel_id=1, replica_groups=mesh['seq'=8,'tp'=4] {'tp'}, use_global_device_ids=true, to_apply=%region_32.33 | all-reduce | flops 4608 | bytes 36864 | tf_op jit(solution)/shard_map/psum | solution.py:291
  1001.1 57.7 %reduce-scatter.8.cloned.1.call-done = bf16[4,300,288]{1,2,0:T(8,128)(2,1)} async-done(((bf16[4,300,1152]{1,2,0:T(8,128)(2,1)}), bf16[4,300,288]{1,2,0:T(8,128)(2,1)}) %reduce-scatter.8.cloned.1.call-update) | async-done | bytes 691216 | tf_op jit(solution)/shard_map/reduce_scatter | solution.py:302
  (301 shorter events, 209.3 us)
Async XLA Ops:
  7.2 52.7 %all-gather.9.cloned.1.call-start = ((), (), s32[]{:S(2)}) async-start(), calls=%async_computation.8 | async-start | bytes 2985984 | tf_op jit(solution)/shard_map/all_gather | solution.py:72
  8.0 78.0 %all-gather.7.cloned.1.call-start = ((), (), s32[]{:S(2)}) async-start(), calls=%async_computation.7 | async-start | bytes 4644864 | tf_op jit(solution)/shard_map/all_gather | solution.py:79
  8.7 114.6 %all-gather.11.cloned.1.call-start = ((), (), s32[]{:S(2)}) async-start(), calls=%async_computation.10 | async-start | bytes 1990656 | tf_op jit(solution)/shard_map/all_gather | solution.py:75
  9.5 188.4 %all-reduce.8.cloned.1.call-start = ((), (), s32[]{:S(2)}) async-start(), calls=%async_computation.9 | async-start | bytes 3538944 | tf_op jit(solution)/shard_map/psum | solution.py:23
  29.7 90.2 %copy-start.9 = (bf16[288,1152]{0,1:T(8,128)(2,1)}, bf16[288,1152]{0,1:T(8,128)(2,1)S(1)}, u32[]{:S(2)}) copy-start(bf16[288,1152]{0,1:T(8,128)(2,1)S(1)} %all_gather.30) | copy-start | bytes 1990660
  43.4 156.5 %copy-start.10 = (bf16[1152,288]{1,0:T(8,128)(2,1)}, bf16[1152,288]{1,0:T(8,128)(2,1)S(1)}, u32[]{:S(2)}) copy-start(bf16[1152,288]{1,0:T(8,128)(2,1)S(1)} %all_gather.32) | copy-start | bytes 1990660
  103.3 182.3 %copy-start.31 = (f32[16,1152]{1,0:T(8,128)}, f32[16,1152]{1,0:T(8,128)S(1)}, u32[]{:S(2)}) copy-start(f32[16,1152]{1,0:T(8,128)S(1)} %get-tuple-element.159) | copy-start | bytes 221188
  103.3 185.1 %copy-start.36 = (f32[16,1152]{1,0:T(8,128)}, f32[16,1152]{1,0:T(8,128)S(1)}, u32[]{:S(2)}) copy-start(f32[16,1152]{1,0:T(8,128)S(1)} %get-tuple-element.154) | copy-start | bytes 221188
  121.9 163.6 %all-reduce.10.cloned.1.call-start = ((), (), s32[]{:S(2)}) async-start(), calls=%async_computation.11 | async-start | bytes 3538944 | tf_op jit(solution)/shard_map/psum | solution.py:23
  210.8 105.8 %all-gather.15.cloned.1.call-start = ((), (), s32[]{:S(2)}) async-start(), calls=%async_computation.13 | async-start | bytes 2985984 | tf_op jit(solution)/shard_map/all_gather | solution.py:78
  211.4 137.4 %all-gather.13.cloned.1.call-start = ((), (), s32[]{:S(2)}) async-start(), calls=%async_computation.12 | async-start | bytes 2985984 | tf_op jit(solution)/shard_map/all_gather | solution.py:77
  212.2 223.0 %all-reduce.12.cloned.1.call-start = ((), (), s32[]{:S(2)}) async-start(), calls=%async_computation.14 | async-start | bytes 3538944 | tf_op jit(solution)/shard_map/psum | solution.py:23
  359.5 176.3 %all-reduce.14.cloned.1.call-start = ((), (), s32[]{:S(2)}) async-start(), calls=%async_computation.15 | async-start | bytes 3538944 | tf_op jit(solution)/shard_map/psum | solution.py:23
  461.1 135.5 %all-reduce.16.cloned.1.call-start = ((), (), s32[]{:S(2)}) async-start(), calls=%async_computation.16 | async-start | bytes 2949120 | tf_op jit(solution)/shard_map/psum | solution.py:278
  469.2 165.4 %reduce-scatter.16.cloned.1.call-start = ((), (), s32[]{:S(2)}) async-start(), calls=%async_computation.21 | async-start | bytes 995328 | tf_op jit(solution)/shard_map/reduce_scatter | solution.py:315
  472.2 200.7 %reduce-scatter.14.cloned.1.call-start = ((), (), s32[]{:S(2)}) async-start(), calls=%async_computation.20 | async-start | bytes 995328 | tf_op jit(solution)/shard_map/reduce_scatter | solution.py:312
  476.0 236.2 %reduce-scatter.12.cloned.1.call-start = ((), (), s32[]{:S(2)}) async-start(), calls=%async_computation.19 | async-start | bytes 995328 | tf_op jit(solution)/shard_map/reduce_scatter | solution.py:309
  547.0 212.3 %reduce-scatter.18.cloned.1.call-start = ((), (), s32[]{:S(2)}) async-start(), calls=%async_computation.22 | async-start | bytes 2985984 | tf_op jit(solution)/shard_map/reduce_scatter | solution.py:318
  551.9 254.9 %reduce-scatter.20.cloned.1.call-start = ((), (), s32[]{:S(2)}) async-start(), calls=%async_computation.23 | async-start | bytes 2985984 | tf_op jit(solution)/shard_map/reduce_scatter | solution.py:321
  556.7 387.1 %all-reduce.18.cloned.1.call-start = ((), (), s32[]{:S(2)}) async-start(), calls=%async_computation.24 | async-start | bytes 7077888 | tf_op jit(solution)/shard_map/psum | solution.py:23
  581.9 417.3 %reduce-scatter.10.cloned.1.call-start = ((), (), s32[]{:S(2)}) async-start(), calls=%async_computation.18 | async-start | bytes 2985984 | tf_op jit(solution)/shard_map/reduce_scatter | solution.py:306
  591.9 466.9 %reduce-scatter.8.cloned.1.call-start = ((), (), s32[]{:S(2)}) async-start(), calls=%async_computation.17 | async-start | bytes 4423680 | tf_op jit(solution)/shard_map/reduce_scatter | solution.py:302
  611.1 332.8 %copy-start.23 = (f32[16,1152]{1,0:T(8,128)S(1)}, f32[16,1152]{1,0:T(8,128)}, u32[]{:S(2)}) copy-start(f32[16,1152]{1,0:T(8,128)} %copy-done.22) | copy-start | bytes 221188
  761.2 184.8 %copy-start.51 = (f32[16,17]{1,0:T(8,128)S(1)}, f32[16,17]{1,0:T(8,128)}, u32[]{:S(2)}) copy-start(f32[16,17]{1,0:T(8,128)} %copy-done.50) | copy-start | bytes 3268
  (60 other events, 465.9 us)
Sparse Core Ops, SparseCore 0:
  10.0 37.6 all-gather.8
  49.5 36.4 all-gather.6
  87.9 26.5 all-gather.10
  122.0 75.7 all-reduce.7
  211.0 74.5 all-reduce.9
  287.3 29.2 all-gather.14
  318.5 30.2 all-gather.12
  359.6 75.5 all-reduce.11
  461.2 74.5 all-reduce.13
  538.9 57.6 all-reduce.15
  600.2 34.3 reduce-scatter.15
  637.7 35.1 reduce-scatter.13
  677.0 35.0 reduce-scatter.11
  715.5 43.7 reduce-scatter.17
  763.0 43.7 reduce-scatter.19
  809.7 134.1 all-reduce.17
  947.2 42.9 reduce-scatter.9
  992.4 66.3 reduce-scatter.7
where the time goes:
time: 1080 us; the launch traced here: 1070 us
  waiting for transfers between devices  733 us (68%)
  matrix products  105 us (10%)
  blocking collectives  95.8 us (9%)
  local copies, waits for them, and re-layouts  71.9 us (7%)
  other arithmetic  45.7 us (4%)
  between operations  15.4 us (1%)
    psum x5, waiting for transfers between devices, total_rows(): return lax.psum(partial_value, 'tp')  407 us
    reduce_scatter x1, waiting for transfers between devices, shards(): lax.psum_scatter(caption_part.astype(jnp.bfloat16), 'tp', scatter_dimensi...  57.7 us
    reduce_scatter x1, waiting for transfers between devices, shards(): lax.psum_scatter(grad_down.astype(jnp.bfloat16), 'seq', scatter_dimension...  45.7 us
    reduce_scatter x1, waiting for transfers between devices, shards(): lax.psum_scatter(grad_up.astype(jnp.bfloat16), 'seq', scatter_dimension=0...  45.6 us
    reduce_scatter x1, waiting for transfers between devices, shards(): lax.psum_scatter(grad_out.astype(jnp.bfloat16), 'seq', scatter_dimension=...  37.7 us
    reduce_scatter x1, waiting for transfers between devices, shards(): lax.psum_scatter(grad_query2.astype(jnp.bfloat16), 'seq', scatter_dimensi...  36.7 us
    all_gather x1, waiting for transfers between devices, shards(): lax.all_gather(w_up, 'seq', axis=0, tiled=True)  28.1 us
    psum x1, blocking collectives, shards(): lax.psum(d_mods.astype(jnp.bfloat16), 'seq').astype(jnp.float32)  24.9 us
  transfers between devices with their start and end apart: 18, of which 15 were waited for; matrix products, arithmetic and copies ran while one was open for 15% of the time, Pallas kernels for 0%

commit v1 on v0

--- a/solution.py
+++ b/solution.py
@@ -8,6 +8,27 @@
 EPSILON = 1e-06
 NEG_FILL = -1e30
 HIGHEST = lax.Precision.HIGHEST
+
+
+def joined_along(blocks, dim):
+    blocks = jnp.moveaxis(blocks, 0, dim)
+    dims = blocks.shape
+    return blocks.reshape(*dims[:dim], dims[dim] * dims[dim + 1], *dims[dim + 2 :])
+
+
+def grow_blocks(x, axis):
+    size, position = (lax.axis_size(axis), lax.axis_index(axis))
+    blocks, stride = (x[None], 1)
+    while stride < size:
+        other = lax.ppermute(blocks, axis, [(i, i ^ stride) for i in range(size)])
+        low = position & stride == 0
+        blocks = jnp.concatenate([jnp.where(low, blocks, other), jnp.where(low, other, blocks)])
+        stride *= 2
+    return blocks
+
+
+def gather_by_bits(x, axis, dim):
+    return joined_along(grow_blocks(x, axis), dim)
 
 
 def normalize(rows):
@@ -76,7 +97,7 @@
         lax.all_gather(w_out2, "seq", axis=1, tiled=True),
         lax.all_gather(w_up, "seq", axis=0, tiled=True),
         lax.all_gather(w_down, "seq", axis=1, tiled=True),
-        lax.all_gather(w_ada, "seq", axis=0, tiled=True),
+        gather_by_bits(w_ada, "seq", 0),
     )
     qkv_matrix = full_qkv.reshape(width, 3 * inner)
     kv_matrix = full_kv2.reshape(width, 2 * inner)

time: 1080 us -> 1120 us (1.037)
  blocking collectives: 95.8 us -> 161 us
  waiting for transfers between devices: 733 us -> 712 us
    all_gather x1, blocking collectives: 13.7 us -> 59.9 us  [shards(): lax.all_gather(w_query2, 'seq', axis=0, tiled=True)]
    all_gather x1 -> x0, waiting for transfers between devices: 21.8 us -> none  [shards(): lax.all_gather(w_ada, 'seq', axis=0, tiled=True)]
    all_gather x1, blocking collectives: 15 us -> 33.1 us  [shards(): lax.all_gather(w_out, 'seq', axis=1, tiled=True)]
  transfers between devices with their start and end apart: 18 -> 20, of which waited for: 15 -> 15; matrix products, arithmetic and copies ran while one was open for 15% -> 14% of each run, Pallas kernels for 0% -> 0%
where the time goes in v1:
time: 1120 us; the launch traced here: 1110 us
  waiting for transfers between devices  712 us (64%)
  blocking collectives  161 us (14%)
  matrix products  101 us (9%)
  local copies, waits for them, and re-layouts  69.2 us (6%)
  other arithmetic  47.2 us (4%)
  between operations  15.2 us (1%)
    psum x5, waiting for transfers between devices, total_rows(): return lax.psum(partial_value, 'tp')  407 us
    all_gather x1, blocking collectives, shards(): lax.all_gather(w_query2, 'seq', axis=0, tiled=True)  59.9 us
    reduce_scatter x1, waiting for transfers between devices, shards(): lax.psum_scatter(caption_part.astype(jnp.bfloat16), 'tp', scatter_dimensi...  57.7 us
    reduce_scatter x1, waiting for transfers between devices, shards(): lax.psum_scatter(grad_up.astype(jnp.bfloat16), 'seq', scatter_dimension=0...  45.7 us
    reduce_scatter x1, waiting for transfers between devices, shards(): lax.psum_scatter(grad_down.astype(jnp.bfloat16), 'seq', scatter_dimension...  45.7 us
    reduce_scatter x1, waiting for transfers between devices, shards(): lax.psum_scatter(grad_out.astype(jnp.bfloat16), 'seq', scatter_dimension=...  37.5 us
    reduce_scatter x1, waiting for transfers between devices, shards(): lax.psum_scatter(grad_query2.astype(jnp.bfloat16), 'seq', scatter_dimensi...  36.8 us
    all_gather x1, blocking collectives, shards(): lax.all_gather(w_out, 'seq', axis=1, tiled=True)  33.1 us
  transfers between devices with their start and end apart: 20, of which 15 were waited for; matrix products, arithmetic and copies ran while one was open for 14% of the time, Pallas kernels for 0%

profile of v1, /device:TPU:0, one launch (start us, length us, event | category | flops | bytes accessed | tf_op | source)
XLA Modules:
  0.0 1111.0 jit_solution(1296536419223416622)
XLA Ops:
  21.8 33.1 %all_gather.26 = bf16[288,1152]{0,1:T(8,128)(2,1)S(1)} all-gather(bf16[288,144]{0,1:T(8,128)(2,1)S(1)} %copy-done.45), channel_id=1, replica_groups=mesh['seq'=8,'tp'=4] {'seq'}, dimensions={1}, use_global_device_ids=true | all-gather | bytes 746496 | tf_op jit(solution)/shard_map/all_gather | solution.py:94
  58.2 59.9 %all_gather.28 = bf16[1152,288]{1,0:T(8,128)(2,1)} all-gather(bf16[144,288]{1,0:T(8,128)(2,1)S(1)} %copy-done.46), channel_id=1, replica_groups=mesh['seq'=8,'tp'=4] {'seq'}, dimensions={0}, use_global_device_ids=true | all-gather | bytes 746496 | tf_op jit(solution)/shard_map/all_gather | solution.py:95
  118.1 11.4 %all_gather.29 = bf16[288,1152]{0,1:T(8,128)(2,1)} all-gather(bf16[288,144]{0,1:T(8,128)(2,1)S(1)} %copy-done.47), channel_id=1, replica_groups=mesh['seq'=8,'tp'=4] {'seq'}, dimensions={1}, use_global_device_ids=true | all-gather | bytes 746496 | tf_op jit(solution)/shard_map/all_gather | solution.py:97
  133.2 13.7 %all-gather = f32[4,1728,4]{1,2,0:T(4,128)S(1)} all-gather(f32[1,1728,4]{1,2,0:T(4,128)S(1)} %convolution_bitcast_fusion), channel_id=1, replica_groups=mesh['seq'=8,'tp'=4] {'tp'}, dimensions={0}, use_global_device_ids=true | all-gather | bytes 138240 | tf_op jit(solution)/shard_map/all_gather | solution.py:106
  166.4 5.6 copy.152
  172.0 5.6 convolution_convert_fusion.4
  177.6 63.3 %all-reduce.8.cloned.1.call-done = f32[16,17,1152]{2,1,0:T(8,128)} async-done(((f32[16,17,1152]{2,1,0:T(8,128)}), f32[16,17,1152]{2,1,0:T(8,128)}) %all-reduce.8.cloned.1.call-update) | async-done | bytes 1253392 | tf_op jit(solution)/shard_map/psum | solution.py:44
  255.1 73.5 %all-reduce.10.cloned.1.call-done = f32[16,17,1152]{2,1,0:T(8,128)} async-done(((f32[16,17,1152]{2,1,0:T(8,128)}), f32[16,17,1152]{2,1,0:T(8,128)}) %all-reduce.10.cloned.1.call-update) | async-done | bytes 1253392 | tf_op jit(solution)/shard_map/psum | solution.py:44
  338.5 21.2 %all-gather.12.cloned.1.call-done = bf16[1152,1152]{0,1:T(8,128)(2,1)} async-done(((bf16[1152,144]{0,1:T(8,128)(2,1)}), bf16[1152,1152]{0,1:T(8,128)(2,1)}) %all-gather.12.cloned.1.call-update) | async-done | bytes 2654224 | tf_op jit(solution)/shard_map/all_gather | solution.py:99
  363.8 28.0 %all-gather.10.cloned.1.call-done = bf16[1152,1152]{1,0:T(8,128)(2,1)} async-done(((bf16[144,1152]{1,0:T(8,128)(2,1)}), bf16[1152,1152]{1,0:T(8,128)(2,1)}) %all-gather.10.cloned.1.call-update) | async-done | bytes 2654224 | tf_op jit(solution)/shard_map/all_gather | solution.py:98
  391.7 5.0 fusion.36
  402.8 75.4 %all-reduce.12.cloned.1.call-done = f32[16,17,1152]{2,1,0:T(8,128)} async-done(((f32[16,17,1152]{2,1,0:T(8,128)}), f32[16,17,1152]{2,1,0:T(8,128)}) %all-reduce.12.cloned.1.call-update) | async-done | bytes 1253392 | tf_op jit(solution)/shard_map/psum | solution.py:44
  518.9 59.8 %all-reduce.14.cloned.1.call-done = f32[16,17,1152]{2,1,0:T(8,128)} async-done(((f32[16,17,1152]{2,1,0:T(8,128)}), f32[16,17,1152]{2,1,0:T(8,128)}) %all-reduce.14.cloned.1.call-update) | async-done | bytes 1253392 | tf_op jit(solution)/shard_map/psum | solution.py:44
  634.8 4.9 all-reduce.16.cloned.1.call-done
  647.5 6.6 convolution_convert_fusion.2
  654.2 23.4 %reduce-scatter.16.cloned.1.call-done = bf16[288,144]{0,1:T(8,128)(2,1)} async-done(((bf16[288,1152]{0,1:T(8,128)(2,1)}), bf16[288,144]{0,1:T(8,128)(2,1)}) %reduce-scatter.16.cloned.1.call-update) | async-done | bytes 82960 | tf_op jit(solution)/shard_map/reduce_scatter | solution.py:336
  679.1 36.8 %reduce-scatter.14.cloned.1.call-done = bf16[144,288]{1,0:T(8,128)(2,1)} async-done(((bf16[1152,288]{1,0:T(8,128)(2,1)}), bf16[144,288]{1,0:T(8,128)(2,1)}) %reduce-scatter.14.cloned.1.call-update) | async-done | bytes 82960 | tf_op jit(solution)/shard_map/reduce_scatter | solution.py:333
  717.5 37.5 %reduce-scatter.12.cloned.1.call-done = bf16[288,144]{0,1:T(8,128)(2,1)} async-done(((bf16[288,1152]{0,1:T(8,128)(2,1)}), bf16[288,144]{0,1:T(8,128)(2,1)}) %reduce-scatter.12.cloned.1.call-update) | async-done | bytes 82960 | tf_op jit(solution)/shard_map/reduce_scatter | solution.py:330
  756.6 45.7 %reduce-scatter.18.cloned.1.call-done = bf16[144,1152]{1,0:T(8,128)(2,1)} async-done(((bf16[1152,1152]{1,0:T(8,128)(2,1)}), bf16[144,1152]{1,0:T(8,128)(2,1)}) %reduce-scatter.18.cloned.1.call-update) | async-done | bytes 331792 | tf_op jit(solution)/shard_map/reduce_scatter | solution.py:339
  804.1 45.7 %reduce-scatter.20.cloned.1.call-done = bf16[1152,144]{0,1:T(8,128)(2,1)} async-done(((bf16[1152,1152]{0,1:T(8,128)(2,1)}), bf16[1152,144]{0,1:T(8,128)(2,1)}) %reduce-scatter.20.cloned.1.call-update) | async-done | bytes 331792 | tf_op jit(solution)/shard_map/reduce_scatter | solution.py:342
  851.6 135.2 %all-reduce.18.cloned.1.call-done = (f32[16,17,1152]{2,1,0:T(8,128)}, f32[16,17,1152]{2,1,0:T(8,128)}) async-done(((f32[16,17,1152]{2,1,0:T(8,128)}, f32[16,17,1152]{2,1,0:T(8,128)}), (f32[16,17,1152]{2,1,0:T(8,128)}, f32[16,17,1152]{2,1,0:T(8,128)})) %all-reduce.18.cloned.1.call-update) | async-done | bytes 2506768 | tf_op jit(solution)/shard_map/psum | solution.py:44
  994.2 24.9 %psum.70 = bf16[4,6912]{1,0:T(4,128)(2,1)S(1)} all-reduce(bf16[4,6912]{1,0:T(4,128)(2,1)S(1)} %bitcast.203), channel_id=1, replica_groups=mesh['seq'=8,'tp'=4] {'seq'}, use_global_device_ids=true, to_apply=%region_31.32 | all-reduce | flops 27648 | bytes 110592 | tf_op jit(solution)/shard_map/psum | solution.py:300
  1022.5 17.6 %psum.71 = f32[4,1152]{1,0:T(4,128)} all-reduce(f32[4,1152]{1,0:T(4,128)S(1)} %fusion.68), channel_id=1, replica_groups=mesh['seq'=8,'tp'=4] {'tp'}, use_global_device_ids=true, to_apply=%region_32.33 | all-reduce | flops 4608 | bytes 36864 | tf_op jit(solution)/shard_map/psum | solution.py:312
  1044.1 57.7 %reduce-scatter.8.cloned.1.call-done = bf16[4,300,288]{1,2,0:T(8,128)(2,1)} async-done(((bf16[4,300,1152]{1,2,0:T(8,128)(2,1)}), bf16[4,300,288]{1,2,0:T(8,128)(2,1)}) %reduce-scatter.8.cloned.1.call-update) | async-done | bytes 691216 | tf_op jit(solution)/shard_map/reduce_scatter | solution.py:323
  (312 shorter events, 204.4 us)
Async XLA Ops:
  7.2 141.5 %all-gather.6.cloned.1.call-start = ((), (), s32[]{:S(2)}) async-start(), calls=%async_computation.7 | async-start | bytes 2985984 | tf_op jit(solution)/shard_map/all_gather | solution.py:93
  7.9 158.5 %all-gather.8.cloned.1.call-start = ((), (), s32[]{:S(2)}) async-start(), calls=%async_computation.9 | async-start | bytes 1990656 | tf_op jit(solution)/shard_map/all_gather | solution.py:96
  8.0 2.3 collective-permute-start
  11.5 43.4 %collective-permute-start.1 = (bf16[2,144,1728]{2,1,0:T(8,128)(2,1)S(1)}, bf16[2,144,1728]{2,1,0:T(8,128)(2,1)}, u32[]{:S(2)}, u32[]{:S(2)}) collective-permute-start(bf16[2,144,1728]{2,1,0:T(8,128)(2,1)S(1)} %pad_maximum_fusion.3), channel_id=1, source_target_pairs={{0,8},{4,12},{8,0},{12,4},{16,24},{20,28},{24,16},{28,20},{1,9},{5... | collective-permute-start | bytes 2985992 | tf_op jit(solution)/shard_map/ppermute | solution.py:23
  14.4 226.4 %all-reduce.8.cloned.1.call-start = ((), (), s32[]{:S(2)}) async-start(), calls=%async_computation.8 | async-start | bytes 3538944 | tf_op jit(solution)/shard_map/psum | solution.py:44
  56.8 73.5 %collective-permute-start.2 = (bf16[4,144,1728]{2,1,0:T(8,128)(2,1)S(1)}, bf16[4,144,1728]{2,1,0:T(8,128)(2,1)S(1)}, u32[]{:S(2)}, u32[]{:S(2)}) collective-permute-start(bf16[4,144,1728]{2,1,0:T(8,128)(2,1)S(1)} %pad_maximum_fusion.1), channel_id=1, source_target_pairs={{0,16},{4,20},{8,24},{12,28},{16,0},{20,4},{24,8},{28,12},{1,17},{... | collective-permute-start | bytes 5971976 | tf_op jit(solution)/shard_map/ppermute | solution.py:23
  148.0 180.7 %copy-start.31 = (f32[16,1152]{1,0:T(8,128)}, f32[16,1152]{1,0:T(8,128)S(1)}, u32[]{:S(2)}) copy-start(f32[16,1152]{1,0:T(8,128)S(1)} %get-tuple-element.165) | copy-start | bytes 221188
  148.0 183.5 %copy-start.36 = (f32[16,1152]{1,0:T(8,128)}, f32[16,1152]{1,0:T(8,128)S(1)}, u32[]{:S(2)}) copy-start(f32[16,1152]{1,0:T(8,128)S(1)} %get-tuple-element.160) | copy-start | bytes 221188
  165.0 163.6 %all-reduce.10.cloned.1.call-start = ((), (), s32[]{:S(2)}) async-start(), calls=%async_computation.10 | async-start | bytes 3538944 | tf_op jit(solution)/shard_map/psum | solution.py:44
  253.9 105.8 %all-gather.12.cloned.1.call-start = ((), (), s32[]{:S(2)}) async-start(), calls=%async_computation.12 | async-start | bytes 2985984 | tf_op jit(solution)/shard_map/all_gather | solution.py:99
  254.5 137.2 %all-gather.10.cloned.1.call-start = ((), (), s32[]{:S(2)}) async-start(), calls=%async_computation.11 | async-start | bytes 2985984 | tf_op jit(solution)/shard_map/all_gather | solution.py:98
  255.1 223.0 %all-reduce.12.cloned.1.call-start = ((), (), s32[]{:S(2)}) async-start(), calls=%async_computation.13 | async-start | bytes 3538944 | tf_op jit(solution)/shard_map/psum | solution.py:44
  402.5 176.3 %all-reduce.14.cloned.1.call-start = ((), (), s32[]{:S(2)}) async-start(), calls=%async_computation.14 | async-start | bytes 3538944 | tf_op jit(solution)/shard_map/psum | solution.py:44
  504.0 135.6 %all-reduce.16.cloned.1.call-start = ((), (), s32[]{:S(2)}) async-start(), calls=%async_computation.15 | async-start | bytes 2949120 | tf_op jit(solution)/shard_map/psum | solution.py:299
  512.1 165.4 %reduce-scatter.16.cloned.1.call-start = ((), (), s32[]{:S(2)}) async-start(), calls=%async_computation.20 | async-start | bytes 995328 | tf_op jit(solution)/shard_map/reduce_scatter | solution.py:336
  515.1 200.8 %reduce-scatter.14.cloned.1.call-start = ((), (), s32[]{:S(2)}) async-start(), calls=%async_computation.19 | async-start | bytes 995328 | tf_op jit(solution)/shard_map/reduce_scatter | solution.py:333
  518.9 236.1 %reduce-scatter.12.cloned.1.call-start = ((), (), s32[]{:S(2)}) async-start(), calls=%async_computation.18 | async-start | bytes 995328 | tf_op jit(solution)/shard_map/reduce_scatter | solution.py:330
  589.9 212.3 %reduce-scatter.18.cloned.1.call-start = ((), (), s32[]{:S(2)}) async-start(), calls=%async_computation.21 | async-start | bytes 2985984 | tf_op jit(solution)/shard_map/reduce_scatter | solution.py:339
  594.9 254.9 %reduce-scatter.20.cloned.1.call-start = ((), (), s32[]{:S(2)}) async-start(), calls=%async_computation.22 | async-start | bytes 2985984 | tf_op jit(solution)/shard_map/reduce_scatter | solution.py:342
  599.7 387.1 %all-reduce.18.cloned.1.call-start = ((), (), s32[]{:S(2)}) async-start(), calls=%async_computation.23 | async-start | bytes 7077888 | tf_op jit(solution)/shard_map/psum | solution.py:44
  624.8 417.4 %reduce-scatter.10.cloned.1.call-start = ((), (), s32[]{:S(2)}) async-start(), calls=%async_computation.17 | async-start | bytes 2985984 | tf_op jit(solution)/shard_map/reduce_scatter | solution.py:327
  634.8 467.0 %reduce-scatter.8.cloned.1.call-start = ((), (), s32[]{:S(2)}) async-start(), calls=%async_computation.16 | async-start | bytes 4423680 | tf_op jit(solution)/shard_map/reduce_scatter | solution.py:323
  654.1 332.7 %copy-start.23 = (f32[16,1152]{1,0:T(8,128)S(1)}, f32[16,1152]{1,0:T(8,128)}, u32[]{:S(2)}) copy-start(f32[16,1152]{1,0:T(8,128)} %copy-done.22) | copy-start | bytes 221188
  804.1 184.9 %copy-start.51 = (f32[16,17]{1,0:T(8,128)S(1)}, f32[16,17]{1,0:T(8,128)}, u32[]{:S(2)}) copy-start(f32[16,17]{1,0:T(8,128)} %copy-done.50) | copy-start | bytes 3268
  (63 other events, 606.6 us)
Sparse Core Ops, SparseCore 0:
  9.9 40.9 all-gather.5
  52.8 36.1 all-gather.7
  165.1 75.6 all-reduce.7
  254.1 74.5 all-reduce.9
  330.4 29.2 all-gather.11
  361.4 30.2 all-gather.9
  402.6 75.4 all-reduce.11
  504.2 74.5 all-reduce.13
  582.0 57.6 all-reduce.15
  643.1 34.3 reduce-scatter.15
  680.8 35.0 reduce-scatter.13
  719.9 35.0 reduce-scatter.11
  758.4 43.7 reduce-scatter.17
  806.0 43.7 reduce-scatter.19
  852.6 134.1 all-reduce.17
  990.2 42.9 reduce-scatter.9
  1035.4 66.3 reduce-scatter.7
